TPU v7x, 32 devices: a whole 2x2x4 slice. The times are simulated.
32 devices in a mesh: head: 4 (over z), tok: 8 (over y, x, core).
Axes of the slice: x: 2, y: 2, z: 4, core: 2. Of those that a mesh axis runs over, the one named last changes fastest.
Arguments:
- video_q: bfloat16 [7168, 2048], P('tok', 'head'), may hold values from -6 to 6
- video_k: bfloat16 [7168, 2048], P('tok', 'head'), may hold values from -6 to 6
- video_v: bfloat16 [7168, 2048], P('tok', 'head'), may hold values from -6 to 6
- audio_q: bfloat16 [256, 2048], P('tok', 'head'), may hold values from -6 to 6
- audio_k: bfloat16 [256, 2048], P('tok', 'head'), may hold values from -6 to 6
- audio_v: bfloat16 [256, 2048], P('tok', 'head'), may hold values from -6 to 6
- norm_gain: float32 [2048], replicated, may hold values from 0.5 to 1.5
Outputs:
- video_out: bfloat16 [7168, 2048], P(('tok', 'head'))
- audio_out: bfloat16 [256, 2048], P('tok', 'head')
All inputs are finite; a program needn't handle non-finite values.
Results may differ from a plain program's by a relative error of at most 0.0095.
Values may be sent and summed in bfloat16 or wider, within the bound.
No kernel may reach another device: no remote copies, remote signals or barrier semaphores. Data moves between devices by JAX's collectives and lax.ppermute only.
A program may use at most 64 MiB of HBM per device.

v0:
```python
import jax
import jax.numpy as jnp
from jax import lax
from jax.sharding import PartitionSpec as P

HEAD_DIM = 64


def shards(video_q, video_k, video_v, audio_q, audio_k, audio_v, norm_gain):
    query_rows, local_width = video_q.shape
    heads_here = local_width // HEAD_DIM
    audio_rows = audio_q.shape[0]
    scaling = HEAD_DIM ** (-0.5)

    def split_heads(matrix):
        return matrix.reshape(matrix.shape[0], heads_here, HEAD_DIM)

    video_heads = split_heads(video_q)
    pieces = (
        lax.all_gather(audio_k, "tok", axis=0, tiled=True),
        lax.all_gather(audio_v, "tok", axis=0, tiled=True),
    )
    running_max = jnp.full((heads_here, query_rows), -1e30, jnp.float32)
    running_sum = jnp.zeros((heads_here, query_rows), jnp.float32)
    running_out = jnp.zeros((heads_here, query_rows, HEAD_DIM), jnp.float32)
    key_block = split_heads(pieces[0])
    value_block = split_heads(pieces[1])
    max_list = []
    sum_list = []
    out_list = []
    for absorb_head_index in range(heads_here):
        absorb_scores = (
            jnp.einsum(
                "qd,kd->qk",
                video_heads[:, absorb_head_index],
                key_block[:, absorb_head_index],
                preferred_element_type=jnp.float32,
            )
            * scaling
        )
        new_max = jnp.maximum(running_max[absorb_head_index], jnp.max(absorb_scores, axis=1))
        absorb_weights = jnp.exp(absorb_scores - new_max[:, None])
        factor = jnp.exp(running_max[absorb_head_index] - new_max)
        sum_list.append(running_sum[absorb_head_index] * factor + jnp.sum(absorb_weights, axis=1))
        out_list.append(
            running_out[absorb_head_index] * factor[:, None]
            + jnp.dot(
                absorb_weights.astype(jnp.bfloat16),
                value_block[:, absorb_head_index],
                preferred_element_type=jnp.float32,
            )
        )
        max_list.append(new_max)
    final_sum = jnp.stack(sum_list)
    final_out = jnp.stack(out_list)
    video_attn = (
        (final_out / final_sum[:, :, None]).transpose(1, 0, 2).reshape(query_rows, local_width)
    )
    video_attn = video_attn.astype(jnp.bfloat16)
    head_count = lax.axis_size("head")
    pieces = video_attn.reshape(head_count, query_rows // head_count, local_width)
    received = lax.all_to_all(pieces, "head", split_axis=0, concat_axis=2, tiled=True)
    normalize_received = received[0]
    widened = normalize_received.astype(jnp.float32)
    mean_square = jnp.mean(widened * widened, axis=-1, keepdims=True)
    video_out = (widened * lax.rsqrt(mean_square + 1e-06) * norm_gain).astype(jnp.bfloat16)
    all_queries = split_heads(lax.all_gather(audio_q, "tok", axis=0, tiled=True))
    video_keys = split_heads(video_k)
    video_values = split_heads(video_v)
    max_list, sum_list, out_list = ([], [], [])
    for head_index in range(heads_here):
        scores = (
            jnp.einsum(
                "qd,kd->qk",
                all_queries[:, head_index],
                video_keys[:, head_index],
                preferred_element_type=jnp.float32,
            )
            * scaling
        )
        local_max = jnp.max(scores, axis=1)
        weights = jnp.exp(scores - local_max[:, None])
        max_list.append(local_max)
        sum_list.append(jnp.sum(weights, axis=1))
        out_list.append(
            jnp.dot(
                weights.astype(jnp.bfloat16),
                video_values[:, head_index],
                preferred_element_type=jnp.float32,
            )
        )
    part_max = jnp.stack(max_list)
    part_sum = jnp.stack(sum_list)
    part_out = jnp.stack(out_list)
    tok_count = lax.axis_size("tok")
    grouped_max = part_max.reshape(heads_here, tok_count, audio_rows)
    grouped_sum = part_sum.reshape(heads_here, tok_count, audio_rows)
    grouped_out = part_out.reshape(heads_here, tok_count, audio_rows, HEAD_DIM)
    got_max, got_sum, got_out = (
        lax.all_to_all(grouped_max, "tok", split_axis=1, concat_axis=1, tiled=True),
        lax.all_to_all(grouped_sum, "tok", split_axis=1, concat_axis=1, tiled=True),
        lax.all_to_all(grouped_out, "tok", split_axis=1, concat_axis=1, tiled=True),
    )
    joint_max = jnp.max(got_max, axis=1, keepdims=True)
    factor = jnp.exp(got_max - joint_max)
    own_sum = jnp.sum(got_sum * factor, axis=1)
    own_out = jnp.sum(got_out * factor[:, :, :, None], axis=1)
    audio_out = (own_out / own_sum[:, :, None]).transpose(1, 0, 2).reshape(audio_rows, local_width)
    return (video_out, audio_out.astype(jnp.bfloat16))


def solution(mesh):
    placed = (
        P("tok", "head"),
        P("tok", "head"),
        P("tok", "head"),
        P("tok", "head"),
        P("tok", "head"),
        P("tok", "head"),
        P(),
    )
    return jax.shard_map(
        shards,
        mesh=mesh,
        in_specs=placed,
        out_specs=(P(("tok", "head"), None), P("tok", "head")),
        check_vma=False,
    )
```

profile of v0, /device:TPU:2, one launch (start us, length us, event | category | flops | bytes accessed | tf_op | source)
XLA Modules:
  0.0 136.5 jit_solution(5439281923956498559)
XLA Ops:
  0.6 1.5 %copy.41 = bf16[896,512]{0,1:T(8,128)(2,1)S(1)} copy(bf16[896,512]{1,0:T(8,128)(2,1)} %param.8) | data formatting | bytes 1835008 | tf_op args[1]
  2.2 9.3 %all_gather.11 = bf16[256,512]{1,0:T(8,128)(2,1)S(1)} all-gather(bf16[32,512]{1,0:T(8,128)(2,1)S(1)} %copy-done.27), channel_id=1, replica_groups=mesh['head'=4,'tok'=8] {'tok'}, dimensions={0}, use_global_device_ids=true | all-gather | bytes 294912 | tf_op jit(solution)/shard_map/all_gather | solution.py:67
  23.2 3.8 %all-to-all-start.2 = ((f32[8,1,256]{2,1,0:T(1,128)}), f32[8,1,256]{2,1,0:T(1,128)S(1)}, u32[]{:S(2)}, u32[]{:S(2)}) async-start(f32[8,1,256]{2,1,0:T(1,128)} %reshape.485), calls=%async_computation.2 | async-start | bytes 16384 | tf_op jit(solution)/shard_map/all_to_all | solution.py:100
  26.9 9.3 %all_gather.9 = bf16[256,512]{1,0:T(8,128)(2,1)S(1)} all-gather(bf16[32,512]{1,0:T(8,128)(2,1)S(1)} %copy-done.28), channel_id=1, replica_groups=mesh['head'=4,'tok'=8] {'tok'}, dimensions={0}, use_global_device_ids=true | all-gather | bytes 294912 | tf_op jit(solution)/shard_map/all_gather | solution.py:20
  44.6 8.5 %all_gather.10 = bf16[256,512]{1,0:T(8,128)(2,1)S(1)} all-gather(bf16[32,512]{1,0:T(8,128)(2,1)S(1)} %copy-done.29), channel_id=1, replica_groups=mesh['head'=4,'tok'=8] {'tok'}, dimensions={0}, use_global_device_ids=true | all-gather | bytes 294912 | tf_op jit(solution)/shard_map/all_gather | solution.py:21
  60.6 1.6 %fusion.44 = (f32[256]{0:T(256)}, bf16[256,896]{1,0:T(8,128)(2,1)}) fusion(f32[256,896]{1,0:T(8,128)S(1)} %copy-done.13, f32[256]{0:T(256)S(1)} %copy-done.48), kind=kLoop, calls=%fused_computation.97 | loop fusion | flops 687872 | bytes 1378304 | tf_op jit(solution)/shard_map/reduce_sum | solution.py:84
  62.2 1.6 %fusion.46 = (f32[256]{0:T(256)}, bf16[256,896]{1,0:T(8,128)(2,1)}) fusion(f32[256,896]{1,0:T(8,128)S(1)} %copy-done.12, f32[256]{0:T(256)S(1)} %copy-done.46), kind=kLoop, calls=%fused_computation.99 | loop fusion | flops 687872 | bytes 1378304 | tf_op jit(solution)/shard_map/reduce_sum | solution.py:84
  63.8 1.6 %fusion.48 = (f32[256]{0:T(256)}, bf16[256,896]{1,0:T(8,128)(2,1)}) fusion(f32[256,896]{1,0:T(8,128)S(1)} %copy-done.11, f32[256]{0:T(256)S(1)} %copy-done.44), kind=kLoop, calls=%fused_computation.101 | loop fusion | flops 687872 | bytes 1378304 | tf_op jit(solution)/shard_map/reduce_sum | solution.py:84
  65.4 1.5 %fusion.50 = (f32[256]{0:T(256)}, bf16[256,896]{1,0:T(8,128)(2,1)}) fusion(f32[256,896]{1,0:T(8,128)S(1)} %copy-done.10, f32[256]{0:T(256)S(1)} %copy-done.42), kind=kLoop, calls=%fused_computation.103 | loop fusion | flops 687872 | bytes 1378304 | tf_op jit(solution)/shard_map/reduce_sum | solution.py:84
  67.0 1.6 %fusion.52 = (f32[256]{0:T(256)}, bf16[256,896]{1,0:T(8,128)(2,1)}) fusion(f32[256,896]{1,0:T(8,128)S(1)} %copy-done.9, f32[256]{0:T(256)S(1)} %copy-done.40), kind=kLoop, calls=%fused_computation.105 | loop fusion | flops 687872 | bytes 1378304 | tf_op jit(solution)/shard_map/reduce_sum | solution.py:84
  68.6 1.6 %fusion.54 = (f32[256]{0:T(256)}, bf16[256,896]{1,0:T(8,128)(2,1)}) fusion(f32[256,896]{1,0:T(8,128)S(1)} %copy-done.8, f32[256]{0:T(256)S(1)} %copy-done.38), kind=kLoop, calls=%fused_computation.107 | loop fusion | flops 687872 | bytes 1378304 | tf_op jit(solution)/shard_map/reduce_sum | solution.py:84
  70.2 1.5 %fusion.56 = (f32[256]{0:T(256)}, bf16[256,896]{1,0:T(8,128)(2,1)}) fusion(f32[256,896]{1,0:T(8,128)S(1)} %copy-done.7, f32[256]{0:T(256)S(1)} %copy-done.36), kind=kLoop, calls=%fused_computation.109 | loop fusion | flops 687872 | bytes 1378304 | tf_op jit(solution)/shard_map/reduce_sum | solution.py:84
  71.7 2.2 %copy.42 = bf16[896,512]{0,1:T(8,128)(2,1)} copy(bf16[896,512]{1,0:T(8,128)(2,1)} %param.9) | data formatting | bytes 1835008 | tf_op args[2]
  73.9 1.6 %fusion.16 = f32[8,896,64]{1,2,0:T(8,128)S(1)} fusion(f32[896,256]{0,1:T(8,128)} %copy-done.5, f32[896]{0:T(1024)S(1)} %broadcast_maximum_fusion.7, f32[896]{0:T(1024)S(1)} %get-tuple-element.35, bf16[256,8,64]{0,2,1:T(8,128)(2,1)S(1)} %bitcast.365), kind=kOutput, calls=%fused_computation.44 | convolution fusion | flops 29876224 | bytes 1187840 | tf_op jit(solution)/shard_map/dot_general | solution.py:47
  75.5 1.5 %fusion.14 = f32[8,896,64]{1,2,0:T(8,128)S(1)} fusion(f32[8,896,64]{1,2,0:T(8,128)S(1)} %fusion.16, f32[896,256]{0,1:T(8,128)} %get-tuple-element.39, f32[896]{0:T(1024)S(1)} %broadcast_maximum_fusion.6, f32[896]{0:T(1024)S(1)} %get-tuple-element.33, bf16[256,8,64]{0,2,1:T(8,128)(2,1)S(1)} %bitcast.366), kind=kOutput, calls=%fused_computation.41 | convolution fusion | flops 29876224 | bytes 1187840 | tf_op jit(solution)/shard_map/dot_general | solution.py:47
  83.7 4.7 %all-to-all-start.3 = ((f32[8,1,256]{2,1,0:T(1,128)}), f32[8,1,256]{2,1,0:T(1,128)S(1)}, u32[]{:S(2)}, u32[]{:S(2)}) async-start(f32[8,1,256]{2,1,0:T(1,128)} %reshape.487), calls=%async_computation.3 | async-start | bytes 16384 | tf_op jit(solution)/shard_map/all_to_all | solution.py:101
  88.7 1.5 %reshape.483 = f32[8,1,16384]{2,1,0:T(1,128)} reshape(f32[8,8,32,64]{3,2,1,0:T(8,128)S(1)} %bitcast.332) | data formatting | bytes 1048576
  90.2 1.5 %all-to-all-done.3 = f32[8,1,256]{2,1,0:T(1,128)S(1)} async-done(((f32[8,1,256]{2,1,0:T(1,128)}), f32[8,1,256]{2,1,0:T(1,128)S(1)}, u32[]{:S(2)}, u32[]{:S(2)}) %all-to-all-start.3) | async-done | bytes 8224 | tf_op jit(solution)/shard_map/all_to_all | solution.py:101
  91.7 4.9 %all-to-all-start.1 = ((f32[8,1,16384]{2,1,0:T(1,128)}), f32[8,1,16384]{2,1,0:T(1,128)S(1)}, u32[]{:S(2)}, u32[]{:S(2)}) async-start(f32[8,1,16384]{2,1,0:T(1,128)} %reshape.483), calls=%async_computation.1 | async-start | bytes 1048576 | tf_op jit(solution)/shard_map/all_to_all | solution.py:102
  97.6 1.7 %fusion.25 = bf16[896,8,64]{0,2,1:T(8,128)(2,1)S(1)} fusion(f32[8,896,64]{1,2,0:T(8,128)} %fusion.2, f32[8,896]{1,0:T(8,128)S(1)} %stack.112), kind=kLoop, calls=%fused_computation.78 | loop fusion | flops 917504 | bytes 2781184 | tf_op jit(solution)/shard_map/convert_element_type | solution.py:59
  101.5 3.4 %all-to-all-done.1 = f32[8,1,16384]{2,1,0:T(1,128)S(1)} async-done(((f32[8,1,16384]{2,1,0:T(1,128)}), f32[8,1,16384]{2,1,0:T(1,128)S(1)}, u32[]{:S(2)}, u32[]{:S(2)}) %all-to-all-start.1) | async-done | bytes 524320 | tf_op jit(solution)/shard_map/all_to_all | solution.py:102
  104.9 4.9 %all-to-all-start = ((bf16[4,224,512]{2,1,0:T(8,128)(2,1)}), bf16[4,224,512]{2,1,0:T(8,128)(2,1)S(1)}, u32[]{:S(2)}, u32[]{:S(2)}) async-start(bf16[4,224,512]{2,1,0:T(8,128)(2,1)} %copy.38), calls=%async_computation | async-start | bytes 1835008 | tf_op jit(solution)/shard_map/all_to_all | solution.py:62
  111.8 1.9 %reduce.5 = f32[8,16384]{1,0:T(8,128)S(1)} reduce(f32[8,1,16384]{2,1,0:T(1,128)S(1)} %all-to-all-done.1, f32[]{:T(128)} %broadcast.428), dimensions={1}, to_apply=%all_to_all.17.reduce_sub_computation | reduce | bytes 1048580 | tf_op jit(solution)/shard_map/all_to_all | solution.py:102
  115.3 17.6 %all-to-all-done = bf16[4,224,512]{2,1,0:T(8,128)(2,1)S(1)} async-done(((bf16[4,224,512]{2,1,0:T(8,128)(2,1)}), bf16[4,224,512]{2,1,0:T(8,128)(2,1)S(1)}, u32[]{:S(2)}, u32[]{:S(2)}) %all-to-all-start) | async-done | bytes 917536 | tf_op jit(solution)/shard_map/all_to_all | solution.py:62
  (230 shorter events, 44.4 us)
Async XLA Ops:
  12.9 8.8 %copy-start.49 = (f32[256]{0:T(256)}, f32[256]{0:T(256)S(1)}, u32[]{:S(2)}) copy-start(f32[256]{0:T(256)S(1)} %get-tuple-element.52) | copy-start | bytes 3076
  14.2 7.7 %copy-start.47 = (f32[256]{0:T(256)}, f32[256]{0:T(256)S(1)}, u32[]{:S(2)}) copy-start(f32[256]{0:T(256)S(1)} %get-tuple-element.54) | copy-start | bytes 3076
  15.5 6.4 %copy-start.45 = (f32[256]{0:T(256)}, f32[256]{0:T(256)S(1)}, u32[]{:S(2)}) copy-start(f32[256]{0:T(256)S(1)} %get-tuple-element.56) | copy-start | bytes 3076
  16.7 5.3 %copy-start.43 = (f32[256]{0:T(256)}, f32[256]{0:T(256)S(1)}, u32[]{:S(2)}) copy-start(f32[256]{0:T(256)S(1)} %get-tuple-element.58) | copy-start | bytes 3076
  18.0 18.2 %copy-start.41 = (f32[256]{0:T(256)}, f32[256]{0:T(256)S(1)}, u32[]{:S(2)}) copy-start(f32[256]{0:T(256)S(1)} %get-tuple-element.60) | copy-start | bytes 3076
  18.0 9.0 %copy-start.28 = (bf16[32,512]{1,0:T(8,128)(2,1)S(1)}, bf16[32,512]{1,0:T(8,128)(2,1)}, u32[]{:S(2)}) copy-start(bf16[32,512]{1,0:T(8,128)(2,1)} %param.11) | copy-start | bytes 98308
  18.0 18.4 %copy-start.26 = (bf16[896,512]{1,0:T(8,128)(2,1)S(1)}, bf16[896,512]{1,0:T(8,128)(2,1)}, u32[]{:S(2)}) copy-start(bf16[896,512]{1,0:T(8,128)(2,1)} %param.7) | copy-start | bytes 2752516
  19.2 17.7 %copy-start.39 = (f32[256]{0:T(256)}, f32[256]{0:T(256)S(1)}, u32[]{:S(2)}) copy-start(f32[256]{0:T(256)S(1)} %get-tuple-element.62) | copy-start | bytes 3076
  20.5 16.5 %copy-start.37 = (f32[256]{0:T(256)}, f32[256]{0:T(256)S(1)}, u32[]{:S(2)}) copy-start(f32[256]{0:T(256)S(1)} %get-tuple-element.64) | copy-start | bytes 3076
  21.7 15.6 %copy-start.35 = (f32[256]{0:T(256)}, f32[256]{0:T(256)S(1)}, u32[]{:S(2)}) copy-start(f32[256]{0:T(256)S(1)} %get-tuple-element.66) | copy-start | bytes 3076
  23.2 60.6 %all-to-all-start.2 = ((f32[8,1,256]{2,1,0:T(1,128)}), f32[8,1,256]{2,1,0:T(1,128)S(1)}, u32[]{:S(2)}, u32[]{:S(2)}) async-start(f32[8,1,256]{2,1,0:T(1,128)} %reshape.485), calls=%async_computation.2 | async-start | bytes 16384 | tf_op jit(solution)/shard_map/all_to_all | solution.py:100
  37.0 5.8 %copy-start.6 = (bf16[896,512]{0,1:T(8,128)(2,1)}, bf16[896,512]{0,1:T(8,128)(2,1)S(1)}, u32[]{:S(2)}) copy-start(bf16[896,512]{0,1:T(8,128)(2,1)S(1)} %copy.35) | copy-start | bytes 2752516
  37.3 7.0 %copy-start.5 = (f32[896,256]{0,1:T(8,128)}, f32[896,256]{0,1:T(8,128)S(1)}, u32[]{:S(2)}) copy-start(f32[896,256]{0,1:T(8,128)S(1)} %get-tuple-element.37) | copy-start | bytes 2752516
  60.6 4.8 %copy-start.10 = (f32[256,896]{1,0:T(8,128)S(1)}, f32[256,896]{1,0:T(8,128)}, u32[]{:S(2)}) copy-start(f32[256,896]{1,0:T(8,128)} %get-tuple-element.61) | copy-start | bytes 2752516
  60.6 4.8 %copy-start.42 = (f32[256]{0:T(256)S(1)}, f32[256]{0:T(256)}, u32[]{:S(2)}) copy-start(f32[256]{0:T(256)} %copy-done.41) | copy-start | bytes 3076
  80.0 8.5 %copy-start.30 = (f32[896]{0:T(1024)S(1)}, f32[896]{0:T(1024)}, u32[]{:S(2)}) copy-start(f32[896]{0:T(1024)} %get-tuple-element.30) | copy-start | bytes 10756
  80.0 8.5 %copy-start.31 = (f32[896]{0:T(1024)S(1)}, f32[896]{0:T(1024)}, u32[]{:S(2)}) copy-start(f32[896]{0:T(1024)} %get-tuple-element.28) | copy-start | bytes 10756
  80.0 8.5 %copy-start.32 = (f32[896]{0:T(1024)S(1)}, f32[896]{0:T(1024)}, u32[]{:S(2)}) copy-start(f32[896]{0:T(1024)} %get-tuple-element.26) | copy-start | bytes 10756
  80.0 8.6 %copy-start.33 = (f32[896]{0:T(1024)S(1)}, f32[896]{0:T(1024)}, u32[]{:S(2)}) copy-start(f32[896]{0:T(1024)} %get-tuple-element.24) | copy-start | bytes 10756
  80.0 8.6 %copy-start.34 = (f32[896]{0:T(1024)S(1)}, f32[896]{0:T(1024)}, u32[]{:S(2)}) copy-start(f32[896]{0:T(1024)} %get-tuple-element.22) | copy-start | bytes 10756
  82.1 6.5 %copy-start.25 = (f32[8,8,32,64]{3,2,1,0:T(8,128)S(1)}, f32[8,8,32,64]{3,2,1,0:T(8,128)}, u32[]{:S(2)}) copy-start(f32[8,8,32,64]{3,2,1,0:T(8,128)} %copy-done.24) | copy-start | bytes 1572868
  83.7 8.0 %all-to-all-start.3 = ((f32[8,1,256]{2,1,0:T(1,128)}), f32[8,1,256]{2,1,0:T(1,128)S(1)}, u32[]{:S(2)}, u32[]{:S(2)}) async-start(f32[8,1,256]{2,1,0:T(1,128)} %reshape.487), calls=%async_computation.3 | async-start | bytes 16384 | tf_op jit(solution)/shard_map/all_to_all | solution.py:101
  91.7 13.1 %all-to-all-start.1 = ((f32[8,1,16384]{2,1,0:T(1,128)}), f32[8,1,16384]{2,1,0:T(1,128)S(1)}, u32[]{:S(2)}, u32[]{:S(2)}) async-start(f32[8,1,16384]{2,1,0:T(1,128)} %reshape.483), calls=%async_computation.1 | async-start | bytes 1048576 | tf_op jit(solution)/shard_map/all_to_all | solution.py:102
  104.9 28.0 %all-to-all-start = ((bf16[4,224,512]{2,1,0:T(8,128)(2,1)}), bf16[4,224,512]{2,1,0:T(8,128)(2,1)S(1)}, u32[]{:S(2)}, u32[]{:S(2)}) async-start(bf16[4,224,512]{2,1,0:T(8,128)(2,1)} %copy.38), calls=%async_computation | async-start | bytes 1835008 | tf_op jit(solution)/shard_map/all_to_all | solution.py:62
  (40 other events, 112.6 us)
where the time goes:
time: 137 us
  blocking collectives  27.1 us (20%)
  other arithmetic  25.6 us (19%)
  matrix products  24.9 us (18%)
  waiting for transfers between devices  22.4 us (16%)
  starting transfers between devices  18.2 us (13%)
  local copies, waits for them, and re-layouts  16.8 us (12%)
  between operations  1.52 us (1%)
    all_to_all x1, waiting for transfers between devices, shards(): lax.all_to_all(pieces, 'head', split_axis=0, concat_axis=2, tiled=True)  17.6 us
    reduce_sum x8, other arithmetic, shards(): sum_list.append(jnp.sum(weights, axis=1))  11.8 us
    dot_general x8, matrix products, shards(): jnp.einsum('qd,kd->qk', all_queries[:, head_index], video_keys[:, head_in...  10.1 us
    unnamed x130, local copies, waits for them, and re-layouts  10 us
    all_gather x1, blocking collectives, shards(): lax.all_gather(audio_q, 'tok', axis=0, tiled=True)  9.31 us
    all_gather x1, blocking collectives, shards(): lax.all_gather(audio_k, 'tok', axis=0, tiled=True)  9.26 us
    all_gather x1, blocking collectives, shards(): lax.all_gather(audio_v, 'tok', axis=0, tiled=True)  8.52 us
    dot_general x8, matrix products, shards(): jnp.einsum('qd,kd->qk', video_heads[:, absorb_head_index], key_block[:, a...  7.34 us
  transfers between devices with their start and end apart: 4, of which 3 were waited for; matrix products, arithmetic and copies ran while one was open for 36% of the time, Pallas kernels for 0%

commit v1 on v0

--- a/solution.py
+++ b/solution.py
@@ -64,7 +64,11 @@
     widened = normalize_received.astype(jnp.float32)
     mean_square = jnp.mean(widened * widened, axis=-1, keepdims=True)
     video_out = (widened * lax.rsqrt(mean_square + 1e-06) * norm_gain).astype(jnp.bfloat16)
-    all_queries = split_heads(lax.all_gather(audio_q, "tok", axis=0, tiled=True))
+    all_queries = split_heads(
+        jnp.concatenate(
+            lax.all_to_all(jnp.stack([audio_q] * lax.axis_size("tok")), "tok", 0, 0), axis=0
+        )
+    )
     video_keys = split_heads(video_k)
     video_values = split_heads(video_v)
     max_list, sum_list, out_list = ([], [], [])

time: 137 us -> 151 us (1.10)
  matrix products: 24.9 us -> 39.9 us
  local copies, waits for them, and re-layouts: 16.8 us -> 31.6 us
  other arithmetic: 25.6 us -> 15.8 us
  blocking collectives: 27.1 us -> 18.3 us
  starting transfers between devices: 18.2 us -> 21.7 us
    reduce_sum x8, other arithmetic: 11.8 us -> 2.38 us  [shards(): sum_list.append(jnp.sum(weights, axis=1))]
    all_gather x1 -> x0, blocking collectives: 9.31 us -> none  [shards(): lax.all_gather(audio_q, 'tok', axis=0, tiled=True)]
    dot_general x8, matrix products: 10.1 us -> 17.2 us  [shards(): jnp.einsum('qd,kd->qk', all_queries[:, head_index], video_keys[:, head_in...]
    slice x0 -> x9, local copies, waits for them, and re-layouts: none -> 6.69 us  [shards(): all_queries[:, head_index]]
    dot_general x8, matrix products: 5.39 us -> 10.2 us  [shards(): jnp.dot(absorb_weights.astype(jnp.bfloat16), value_block[:, absorb_head_i...]
    all_to_all x0 -> x1, starting transfers between devices: none -> 4.25 us  [shards(): lax.all_to_all(jnp.stack([audio_q] * lax.axis_size('tok')), 'tok', 0, 0)]
    another operation x9, local copies, waits for them, and re-layouts: 0.73 us -> 3.82 us  [shards(): part_max = jnp.stack(max_list)]
    dot_general x8, matrix products: 7.34 us -> 9.68 us  [shards(): jnp.einsum('qd,kd->qk', video_heads[:, absorb_head_index], key_block[:, a...]
  transfers between devices with their start and end apart: 4 -> 5, of which waited for: 3 -> 2; matrix products, arithmetic and copies ran while one was open for 36% -> 34% of each run, Pallas kernels for 0% -> 0%
where the time goes in v1:
time: 151 us; the launch traced here: 150 us
  matrix products  39.9 us (26%)
  local copies, waits for them, and re-layouts  31.6 us (21%)
  starting transfers between devices  21.7 us (14%)
  waiting for transfers between devices  20.9 us (14%)
  blocking collectives  18.3 us (12%)
  other arithmetic  15.8 us (10%)
    all_to_all x1, waiting for transfers between devices, shards(): lax.all_to_all(pieces, 'head', split_axis=0, concat_axis=2, tiled=True)  17.6 us
    dot_general x8, matrix products, shards(): jnp.einsum('qd,kd->qk', all_queries[:, head_index], video_keys[:, head_in...  17.2 us
    unnamed x72, local copies, waits for them, and re-layouts  11.6 us
    dot_general x8, matrix products, shards(): jnp.dot(absorb_weights.astype(jnp.bfloat16), value_block[:, absorb_head_i...  10.2 us
    dot_general x8, matrix products, shards(): jnp.einsum('qd,kd->qk', video_heads[:, absorb_head_index], key_block[:, a...  9.68 us
    all_gather x1, blocking collectives, shards(): lax.all_gather(audio_k, 'tok', axis=0, tiled=True)  9.24 us
    all_gather x1, blocking collectives, shards(): lax.all_gather(audio_v, 'tok', axis=0, tiled=True)  9.09 us
    slice x9, local copies, waits for them, and re-layouts, shards(): all_queries[:, head_index]  6.69 us
  transfers between devices with their start and end apart: 5, of which 2 were waited for; matrix products, arithmetic and copies ran while one was open for 34% of the time, Pallas kernels for 0%

profile of v1, /device:TPU:2, one launch (start us, length us, event | category | flops | bytes accessed | tf_op | source)
XLA Modules:
  0.0 149.6 jit_solution(4969228575760090375)
XLA Ops:
  2.2 4.3 %all-to-all-start.1 = ((bf16[8,32,512]{2,1,0:T(8,128)(2,1)}), bf16[8,32,512]{2,1,0:T(8,128)(2,1)S(1)}, u32[]{:S(2)}, u32[]{:S(2)}) async-start(bf16[8,32,512]{2,1,0:T(8,128)(2,1)} %stack.124), calls=%async_computation.1 | async-start | bytes 524288 | tf_op jit(solution)/shard_map/all_to_all | solution.py:69
  6.5 9.2 %all_gather.6 = bf16[256,512]{1,0:T(8,128)(2,1)S(1)} all-gather(bf16[32,512]{1,0:T(8,128)(2,1)} %param.11), channel_id=1, replica_groups=mesh['head'=4,'tok'=8] {'tok'}, dimensions={0}, use_global_device_ids=true | all-gather | bytes 294912 | tf_op jit(solution)/shard_map/all_gather | solution.py:20
  16.8 1.9 %fusion.93 = (f32[896]{0:T(1024)}, f32[896,256]{0,1:T(8,128)}) fusion(bf16[256,8,64]{0,2,1:T(8,128)(2,1)S(1)} %bitcast.373, bf16[896,8,64]{0,2,1:T(8,128)(2,1)S(1)} %bitcast.341), kind=kOutput, calls=%fused_computation.198 | convolution fusion | flops 29817984 | bytes 1068544 | tf_op jit(solution)/shard_map/qd,kd->qk/dot_general | solution.py:33
  18.7 1.9 %fusion.94 = (f32[896]{0:T(1024)}, f32[896,256]{0,1:T(8,128)}) fusion(bf16[256,8,64]{0,2,1:T(8,128)(2,1)S(1)} %bitcast.374, bf16[896,8,64]{0,2,1:T(8,128)(2,1)S(1)} %bitcast.342), kind=kOutput, calls=%fused_computation.199 | convolution fusion | flops 29817984 | bytes 1068544 | tf_op jit(solution)/shard_map/qd,kd->qk/dot_general | solution.py:33
  20.6 1.9 %fusion.95 = (f32[896]{0:T(1024)}, f32[896,256]{0,1:T(8,128)}) fusion(bf16[256,8,64]{0,2,1:T(8,128)(2,1)S(1)} %bitcast.375, bf16[896,8,64]{0,2,1:T(8,128)(2,1)S(1)} %bitcast.343), kind=kOutput, calls=%fused_computation.200 | convolution fusion | flops 29817984 | bytes 1068544 | tf_op jit(solution)/shard_map/qd,kd->qk/dot_general | solution.py:33
  22.4 1.8 %fusion.96 = (f32[896]{0:T(1024)}, f32[896,256]{0,1:T(8,128)}) fusion(bf16[256,8,64]{0,2,1:T(8,128)(2,1)S(1)} %bitcast.376, bf16[896,8,64]{0,2,1:T(8,128)(2,1)S(1)} %bitcast.344), kind=kOutput, calls=%fused_computation.201 | convolution fusion | flops 29817984 | bytes 1068544 | tf_op jit(solution)/shard_map/qd,kd->qk/dot_general | solution.py:33
  27.0 9.1 %all_gather.7 = bf16[256,512]{1,0:T(8,128)(2,1)S(1)} all-gather(bf16[32,512]{1,0:T(8,128)(2,1)S(1)} %copy-done.20), channel_id=1, replica_groups=mesh['head'=4,'tok'=8] {'tok'}, dimensions={0}, use_global_device_ids=true | all-gather | bytes 294912 | tf_op jit(solution)/shard_map/all_gather | solution.py:21
  42.1 2.2 %copy.62 = bf16[896,512]{0,1:T(8,128)(2,1)} copy(bf16[896,512]{1,0:T(8,128)(2,1)} %param.8) | data formatting | bytes 1835008 | tf_op args[1]
  44.4 2.2 %copy.63 = bf16[896,512]{0,1:T(8,128)(2,1)} copy(bf16[896,512]{1,0:T(8,128)(2,1)} %param.9) | data formatting | bytes 1835008 | tf_op args[2]
  46.6 2.3 %fusion.16 = f32[8,896,64]{1,2,0:T(8,128)} fusion(f32[896,256]{0,1:T(8,128)} %copy-done.5, f32[896]{0:T(1024)S(1)} %broadcast_maximum_fusion.7, f32[896]{0:T(1024)S(1)} %copy-done.21, bf16[256,8,64]{0,2,1:T(8,128)(2,1)S(1)} %bitcast.364), kind=kOutput, calls=%fused_computation.44 | convolution fusion | flops 29876224 | bytes 1187840 | tf_op jit(solution)/shard_map/dot_general | solution.py:47
  48.8 2.2 %fusion.14 = f32[8,896,64]{1,2,0:T(8,128)} fusion(f32[8,896,64]{1,2,0:T(8,128)} %fusion.16, f32[896,256]{0,1:T(8,128)} %get-tuple-element.47, f32[896]{0:T(1024)S(1)} %broadcast_maximum_fusion.6, f32[896]{0:T(1024)S(1)} %get-tuple-element.41, bf16[256,8,64]{0,2,1:T(8,128)(2,1)S(1)} %bitcast.365), kind=kOutput, calls=%fused_computation.41 | convolution fusion | flops 29876224 | bytes 1187840 | tf_op jit(solution)/shard_map/dot_general | solution.py:47
  64.8 2.7 %fusion.102 = (f32[256]{0:T(256)}, f32[256,896]{1,0:T(8,128)}) fusion(bf16[896,8,64]{0,2,1:T(8,128)(2,1)} %bitcast.334, bf16[256,1,64]{0,2,1:T(8,128)(2,1)} %copy.65), kind=kOutput, calls=%fused_computation.207 | convolution fusion | flops 29818624 | bytes 1065984 | tf_op jit(solution)/shard_map/qd,kd->qk/dot_general | solution.py:77
  70.4 2.7 %fusion.103 = (f32[256]{0:T(256)}, f32[256,896]{1,0:T(8,128)}) fusion(bf16[896,8,64]{0,2,1:T(8,128)(2,1)} %bitcast.335, bf16[256,1,64]{0,2,1:T(8,128)(2,1)} %copy.66), kind=kOutput, calls=%fused_computation.208 | convolution fusion | flops 29818624 | bytes 1065984 | tf_op jit(solution)/shard_map/qd,kd->qk/dot_general | solution.py:77
  75.2 2.2 %fusion.104 = (f32[256]{0:T(256)S(1)}, f32[256,896]{1,0:T(8,128)}) fusion(bf16[896,8,64]{0,2,1:T(8,128)(2,1)} %bitcast.336, bf16[256,1,64]{0,2,1:T(8,128)(2,1)} %copy.67), kind=kOutput, calls=%fused_computation.209 | convolution fusion | flops 29818624 | bytes 1065984 | tf_op jit(solution)/shard_map/qd,kd->qk/dot_general | solution.py:77
  77.6 2.2 %fusion.105 = (f32[256]{0:T(256)S(1)}, f32[256,896]{1,0:T(8,128)}) fusion(bf16[896,8,64]{0,2,1:T(8,128)(2,1)} %bitcast.337, bf16[256,1,64]{0,2,1:T(8,128)(2,1)S(1)} %copy.68), kind=kOutput, calls=%fused_computation.210 | convolution fusion | flops 29818624 | bytes 1065984 | tf_op jit(solution)/shard_map/qd,kd->qk/dot_general | solution.py:77
  80.0 2.2 %fusion.106 = (f32[256]{0:T(256)S(1)}, f32[256,896]{1,0:T(8,128)}) fusion(bf16[896,8,64]{0,2,1:T(8,128)(2,1)} %bitcast.338, bf16[256,1,64]{0,2,1:T(8,128)(2,1)S(1)} %copy.69), kind=kOutput, calls=%fused_computation.211 | convolution fusion | flops 29818624 | bytes 1065984 | tf_op jit(solution)/shard_map/qd,kd->qk/dot_general | solution.py:77
  82.3 2.1 %fusion.107 = (f32[256]{0:T(256)S(1)}, f32[256,896]{1,0:T(8,128)}) fusion(bf16[896,8,64]{0,2,1:T(8,128)(2,1)} %bitcast.339, bf16[256,1,64]{0,2,1:T(8,128)(2,1)S(1)} %copy.70), kind=kOutput, calls=%fused_computation.212 | convolution fusion | flops 29818624 | bytes 1065984 | tf_op jit(solution)/shard_map/qd,kd->qk/dot_general | solution.py:77
  85.3 3.9 %all-to-all-start.3 = ((f32[8,1,256]{2,1,0:T(1,128)}), f32[8,1,256]{2,1,0:T(1,128)S(1)}, u32[]{:S(2)}, u32[]{:S(2)}) async-start(f32[8,1,256]{2,1,0:T(1,128)} %reshape.483), calls=%async_computation.3 | async-start | bytes 16384 | tf_op jit(solution)/shard_map/all_to_all | solution.py:104
  97.3 4.2 %all-to-all-start.4 = ((f32[8,1,256]{2,1,0:T(1,128)}), f32[8,1,256]{2,1,0:T(1,128)S(1)}, u32[]{:S(2)}, u32[]{:S(2)}) async-start(f32[8,1,256]{2,1,0:T(1,128)} %reshape.485), calls=%async_computation.4 | async-start | bytes 16384 | tf_op jit(solution)/shard_map/all_to_all | solution.py:105
  105.3 4.4 %all-to-all-start.2 = ((f32[8,1,16384]{2,1,0:T(1,128)}), f32[8,1,16384]{2,1,0:T(1,128)S(1)}, u32[]{:S(2)}, u32[]{:S(2)}) async-start(f32[8,1,16384]{2,1,0:T(1,128)} %reshape.481), calls=%async_computation.2 | async-start | bytes 1048576 | tf_op jit(solution)/shard_map/all_to_all | solution.py:106
  114.6 3.4 %all-to-all-done.2 = f32[8,1,16384]{2,1,0:T(1,128)S(1)} async-done(((f32[8,1,16384]{2,1,0:T(1,128)}), f32[8,1,16384]{2,1,0:T(1,128)S(1)}, u32[]{:S(2)}, u32[]{:S(2)}) %all-to-all-start.2) | async-done | bytes 524320 | tf_op jit(solution)/shard_map/all_to_all | solution.py:106
  118.0 4.9 %all-to-all-start = ((bf16[4,224,512]{2,1,0:T(8,128)(2,1)}), bf16[4,224,512]{2,1,0:T(8,128)(2,1)S(1)}, u32[]{:S(2)}, u32[]{:S(2)}) async-start(bf16[4,224,512]{2,1,0:T(8,128)(2,1)} %copy.59), calls=%async_computation | async-start | bytes 1835008 | tf_op jit(solution)/shard_map/all_to_all | solution.py:62
  124.9 1.9 %reduce.5 = f32[8,16384]{1,0:T(8,128)S(1)} reduce(f32[8,1,16384]{2,1,0:T(1,128)S(1)} %all-to-all-done.2, f32[]{:T(128)} %broadcast.430), dimensions={1}, to_apply=%all_to_all.21.reduce_sub_computation | reduce | bytes 1048580 | tf_op jit(solution)/shard_map/all_to_all | solution.py:106
  128.4 17.6 %all-to-all-done = bf16[4,224,512]{2,1,0:T(8,128)(2,1)S(1)} async-done(((bf16[4,224,512]{2,1,0:T(8,128)(2,1)}), bf16[4,224,512]{2,1,0:T(8,128)(2,1)S(1)}, u32[]{:S(2)}, u32[]{:S(2)}) %all-to-all-start) | async-done | bytes 917536 | tf_op jit(solution)/shard_map/all_to_all | solution.py:62
  (183 shorter events, 55.0 us)
Async XLA Ops:
  0.6 15.2 %copy-start.15 = (bf16[896,512]{1,0:T(8,128)(2,1)S(1)}, bf16[896,512]{1,0:T(8,128)(2,1)}, u32[]{:S(2)}) copy-start(bf16[896,512]{1,0:T(8,128)(2,1)} %param.7) | copy-start | bytes 2752516
  2.2 54.3 %all-to-all-start.1 = ((bf16[8,32,512]{2,1,0:T(8,128)(2,1)}), bf16[8,32,512]{2,1,0:T(8,128)(2,1)S(1)}, u32[]{:S(2)}, u32[]{:S(2)}) async-start(bf16[8,32,512]{2,1,0:T(8,128)(2,1)} %stack.124), calls=%async_computation.1 | async-start | bytes 524288 | tf_op jit(solution)/shard_map/all_to_all | solution.py:69
  16.5 8.1 %copy-start.6 = (bf16[896,512]{0,1:T(8,128)(2,1)}, bf16[896,512]{0,1:T(8,128)(2,1)S(1)}, u32[]{:S(2)}) copy-start(bf16[896,512]{0,1:T(8,128)(2,1)S(1)} %copy.56) | copy-start | bytes 2752516
  16.8 9.4 %copy-start.5 = (f32[896,256]{0,1:T(8,128)}, f32[896,256]{0,1:T(8,128)S(1)}, u32[]{:S(2)}) copy-start(f32[896,256]{0,1:T(8,128)S(1)} %get-tuple-element.45) | copy-start | bytes 2752516
  24.3 2.7 %copy-start.20 = (bf16[32,512]{1,0:T(8,128)(2,1)S(1)}, bf16[32,512]{1,0:T(8,128)(2,1)}, u32[]{:S(2)}) copy-start(bf16[32,512]{1,0:T(8,128)(2,1)} %param.12) | copy-start | bytes 98308
  36.2 4.9 %copy-start.19 = (f32[896]{0:T(1024)S(1)}, f32[896]{0:T(1024)}, u32[]{:S(2)}) copy-start(f32[896]{0:T(1024)} %get-tuple-element.48) | copy-start | bytes 10756
  36.2 4.9 %copy-start.18 = (f32[896]{0:T(1024)S(1)}, f32[896]{0:T(1024)}, u32[]{:S(2)}) copy-start(f32[896]{0:T(1024)} %get-tuple-element.50) | copy-start | bytes 10756
  36.2 4.9 %copy-start.2 = (f32[896,256]{0,1:T(8,128)S(1)}, f32[896,256]{0,1:T(8,128)}, u32[]{:S(2)}) copy-start(f32[896,256]{0,1:T(8,128)} %get-tuple-element.51) | copy-start | bytes 2752516
  36.2 5.1 %copy-start.17 = (f32[896]{0:T(1024)S(1)}, f32[896]{0:T(1024)}, u32[]{:S(2)}) copy-start(f32[896]{0:T(1024)} %get-tuple-element.52) | copy-start | bytes 10756
  36.2 5.1 %copy-start = (f32[896,256]{0,1:T(8,128)S(1)}, f32[896,256]{0,1:T(8,128)}, u32[]{:S(2)}) copy-start(f32[896,256]{0,1:T(8,128)} %get-tuple-element.53) | copy-start | bytes 2752516
  42.1 4.4 %copy-start.21 = (f32[896]{0:T(1024)S(1)}, f32[896]{0:T(1024)}, u32[]{:S(2)}) copy-start(f32[896]{0:T(1024)} %get-tuple-element.43) | copy-start | bytes 10756
  46.6 4.5 %copy-start.4 = (f32[896,256]{0,1:T(8,128)S(1)}, f32[896,256]{0,1:T(8,128)}, u32[]{:S(2)}) copy-start(f32[896,256]{0,1:T(8,128)} %get-tuple-element.49) | copy-start | bytes 2752516
  46.6 5.5 %copy-start.3 = (f32[896,256]{0,1:T(8,128)S(1)}, f32[896,256]{0,1:T(8,128)}, u32[]{:S(2)}) copy-start(f32[896,256]{0,1:T(8,128)} %get-tuple-element.51) | copy-start | bytes 2752516
  48.8 4.1 %copy-start.1 = (f32[896,256]{0,1:T(8,128)S(1)}, f32[896,256]{0,1:T(8,128)}, u32[]{:S(2)}) copy-start(f32[896,256]{0,1:T(8,128)} %get-tuple-element.53) | copy-start | bytes 2752516
  77.5 7.1 %copy-start.22 = (f32[1,8,32]{2,0,1:T(1,128)S(1)}, f32[1,8,32]{2,0,1:T(1,128)}, u32[]{:S(2)}) copy-start(f32[1,8,32]{2,0,1:T(1,128)} %stack.128) | copy-start | bytes 3076
  77.5 7.1 %copy-start.23 = (f32[1,8,32]{2,0,1:T(1,128)S(1)}, f32[1,8,32]{2,0,1:T(1,128)}, u32[]{:S(2)}) copy-start(f32[1,8,32]{2,0,1:T(1,128)} %stack.129) | copy-start | bytes 3076
  77.6 11.7 %copy-start.26 = (f32[256]{0:T(256)S(1)}, f32[256]{0:T(256)}, u32[]{:S(2)}) copy-start(f32[256]{0:T(256)} %copy-done.25) | copy-start | bytes 3076
  79.9 9.6 %copy-start.27 = (f32[256]{0:T(256)S(1)}, f32[256]{0:T(256)}, u32[]{:S(2)}) copy-start(f32[256]{0:T(256)} %get-tuple-element.62) | copy-start | bytes 3076
  82.3 7.6 %copy-start.28 = (f32[256]{0:T(256)S(1)}, f32[256]{0:T(256)}, u32[]{:S(2)}) copy-start(f32[256]{0:T(256)} %get-tuple-element.64) | copy-start | bytes 3076
  85.3 12.1 %all-to-all-start.3 = ((f32[8,1,256]{2,1,0:T(1,128)}), f32[8,1,256]{2,1,0:T(1,128)S(1)}, u32[]{:S(2)}, u32[]{:S(2)}) async-start(f32[8,1,256]{2,1,0:T(1,128)} %reshape.483), calls=%async_computation.3 | async-start | bytes 16384 | tf_op jit(solution)/shard_map/all_to_all | solution.py:104
  97.3 7.9 %all-to-all-start.4 = ((f32[8,1,256]{2,1,0:T(1,128)}), f32[8,1,256]{2,1,0:T(1,128)S(1)}, u32[]{:S(2)}, u32[]{:S(2)}) async-start(f32[8,1,256]{2,1,0:T(1,128)} %reshape.485), calls=%async_computation.4 | async-start | bytes 16384 | tf_op jit(solution)/shard_map/all_to_all | solution.py:105
  103.8 6.8 %copy-start.16 = (f32[8,896]{1,0:T(8,128)S(1)}, f32[8,896]{1,0:T(8,128)}, u32[]{:S(2)}) copy-start(f32[8,896]{1,0:T(8,128)} %stack.123) | copy-start | bytes 86020
  105.3 12.7 %all-to-all-start.2 = ((f32[8,1,16384]{2,1,0:T(1,128)}), f32[8,1,16384]{2,1,0:T(1,128)S(1)}, u32[]{:S(2)}, u32[]{:S(2)}) async-start(f32[8,1,16384]{2,1,0:T(1,128)} %reshape.481), calls=%async_computation.2 | async-start | bytes 1048576 | tf_op jit(solution)/shard_map/all_to_all | solution.py:106
  118.0 28.0 %all-to-all-start = ((bf16[4,224,512]{2,1,0:T(8,128)(2,1)}), bf16[4,224,512]{2,1,0:T(8,128)(2,1)S(1)}, u32[]{:S(2)}, u32[]{:S(2)}) async-start(bf16[4,224,512]{2,1,0:T(8,128)(2,1)} %copy.59), calls=%async_computation | async-start | bytes 1835008 | tf_op jit(solution)/shard_map/all_to_all | solution.py:62
  (12 other events, 16.2 us)
